TPU v7x, 32 devices: a whole 2x2x4 slice. The times are simulated.
32 devices in a mesh: row: 16 (over z, y, x), col: 2 (over core).
Axes of the slice: x: 2, y: 2, z: 4, core: 2. Of those that a mesh axis runs over, the one named last changes fastest.
Arguments:
- tsdf_prior: float32 [512, 64, 256], P('row', None, 'col'), may hold values from -1 to 1
- prior_weight: float32 [512, 64, 256], P('row', None, 'col'), may hold values from 0.5 to 8
- depth_maps: float32 [16, 131072], P('row'), may hold values from 0 to 64
- confidence: float32 [16, 131072], P('row'), may hold values from 0.2 to 5
- frustum_tiles: int32 [32, 32, 2], P(('row', 'col')), may hold values from -1 to 31, as said below
- pixel_index: int32 [32, 32, 2, 128], P(('row', 'col')), may hold values from 0 to 131071
- conv_weights: bfloat16 [3, 64, 16, 3, 3], replicated, may hold values from -0.5 to 0.5
Outputs:
- refined: float32 [512, 64, 256], P('row', None, 'col')
- new_weight: float32 [512, 64, 256], P('row', None, 'col')
Inputs may be any that keep to these rules, and one draw needn't show every extreme that they name: `frustum_tiles`: -1 marks an empty slot; otherwise the entry is one of the owner's 32 tiles, and slot s names a tile from the s-th of 2 equal runs of tile numbers.
All inputs are finite; a program needn't handle non-finite values.
Results may differ from a plain program's by a relative error of at most 0.003.
Values may be sent and summed in bfloat16 or wider, within the bound.
A program may use at most 128 MiB of HBM per device.

v0:
```python
import functools

import jax
import jax.numpy as jnp
from jax import lax
from jax.experimental import pallas as pl
from jax.experimental.pallas import tpu as pltpu
from jax.sharding import PartitionSpec as P

GROUPS = 4
TRUNC = 4
LANES = 128
VMEM = pltpu.VMEM


def vmem_specs(count):
    return [pl.BlockSpec(memory_space=VMEM)] * count


def sample_kernel(places_ref, depth_ref, conf_ref, want_ref, got_ref, ids_ref, table_ref, staged_ref,
                  send_sems, recv_sems):
    owners, cap, _ = places_ref.shape
    depth_rows = depth_ref.shape[0]
    split = lax.axis_size("col")
    me = lax.axis_index("row") * split + lax.axis_index("col")
    barrier = pltpu.get_barrier_semaphore()

    def wrapped(place):
        return jnp.where(place >= owners, place - owners, place)

    def coordinates(place):
        return (place // split, place % split)

    def greet(k, carry):
        pl.semaphore_signal(barrier, inc=1, device_id=coordinates(wrapped(me + 1 + k)),
                            device_id_type=pl.DeviceIdType.MESH)
        return carry

    lax.fori_loop(0, owners - 1, greet, 0)
    for at in range(0, depth_rows, LANES):
        block = depth_ref[at : at + LANES, :].T
        high = block.astype(jnp.bfloat16)
        table_ref[0:LANES, at : at + LANES] = high
        table_ref[LANES : 2 * LANES, at : at + LANES] = (block - high.astype(jnp.float32)).astype(jnp.bfloat16)
        table_ref[2 * LANES : 3 * LANES, at : at + LANES] = conf_ref[at : at + LANES, :].T.astype(jnp.bfloat16)
    want = want_ref[...].astype(jnp.float32)
    listed_by = lax.broadcasted_iota(jnp.int32, want.shape, 1)
    wide = cap * LANES

    def compute(k):
        owner = wrapped(me + 1 + k)
        listed = places_ref[owner]
        index = jnp.concatenate([listed[s : s + 1, :] for s in range(cap)], axis=1)
        row = index // LANES
        lane = index % LANES
        hot = (lax.broadcasted_iota(jnp.int32, (depth_rows, wide), 0) == row)
        hot = hot.astype(jnp.float32).astype(jnp.bfloat16)
        found = jnp.dot(table_ref[...], hot, preferred_element_type=jnp.float32)
        chosen = lax.broadcasted_iota(jnp.int32, (LANES, wide), 0) == lane
        results = []
        for value in (found[0:LANES] + found[LANES : 2 * LANES], found[2 * LANES : 3 * LANES]):
            value = jnp.sum(jnp.where(chosen, value, 0.0), axis=0, keepdims=True)
            results += [value[:, s * LANES : (s + 1) * LANES] for s in range(cap)]
        tile = jnp.sum(jnp.where(listed_by == owner, want, 0.0), axis=1, keepdims=True)
        results.append(jnp.broadcast_to(tile, (cap, LANES)))
        return owner, jnp.concatenate(results, axis=0)

    def copy(k):
        owner = wrapped(me + 1 + k)
        return pltpu.make_async_remote_copy(
            src_ref=staged_ref.at[owner], dst_ref=got_ref.at[me],
            send_sem=send_sems.at[k], recv_sem=recv_sems.at[k],
            device_id=coordinates(owner), device_id_type=pl.DeviceIdType.MESH)

    def arrival(k):
        sender = wrapped(me + owners - 1 - k)
        return pltpu.make_async_remote_copy(
            src_ref=staged_ref.at[sender], dst_ref=got_ref.at[sender],
            send_sem=send_sems.at[k], recv_sem=recv_sems.at[k],
            device_id=coordinates(sender), device_id_type=pl.DeviceIdType.MESH)

    def stage(k):
        pairs = [compute(k), compute(k + 1)]
        for owner, value in pairs:
            staged_ref[owner] = value

    stage(0)
    pl.semaphore_wait(barrier, owners - 1)

    def step(p, carry):
        copy(2 * p - 2).start()
        copy(2 * p - 1).start()
        stage(2 * p)
        return carry

    lax.fori_loop(1, owners // 2, step, 0)
    copy(owners - 2).start()
    got_ref[me] = staged_ref[me]

    def drain(k, carry):
        copy(k).wait_send()
        arrival(k).wait_recv()
        return carry

    lax.fori_loop(0, owners - 1, drain, 0)
    ids_ref[...] = got_ref[:, 2 * cap : 3 * cap, :].astype(jnp.int32)


def join_kernel(halo, ids_ref, side_ref, got_ref, prior_ref, weight_ref, joined_ref, total_ref, packed_ref):
    tiles, bins, cols = prior_ref.shape
    readers, rows, _ = got_ref.shape
    cap = rows // 3

    def begin(t, carry):
        weight = weight_ref[t]
        total_ref[t] = weight
        joined_ref[t] = weight * prior_ref[t]
        return carry

    lax.fori_loop(0, tiles, begin, 0, unroll=4)
    levels = lax.broadcasted_iota(jnp.int32, (bins, cols), 0).astype(jnp.float32)

    batch = 2

    def add(step, carry):
        terms = []
        for one in range(batch):
            reader = step * batch + one
            for s in range(cap):
                listed = ids_ref[reader, s, 0]
                tile = jnp.maximum(listed, 0)
                height = got_ref[reader, s : s + 1, :]
                sure = got_ref[reader, cap + s : cap + s + 1, :]
                sure = jnp.where(listed >= 0, sure, 0.0)
                scaled = (height - levels) * (1.0 / TRUNC)
                signed = jnp.clip(scaled, -1.0, 1.0)
                visible = jnp.clip(scaled + 2.0, 0.0, 1.0)
                miss = signed - prior_ref[tile]
                observed = sure * visible / (1.0 + 4.0 * miss * miss)
                terms.append((tile, observed, observed * signed))
        for tile, observed, weighted in terms:
            total_ref[tile] += observed
            joined_ref[tile] += weighted
        return carry

    lax.fori_loop(0, readers // batch, add, 0)
    place = lax.broadcasted_iota(jnp.int32, (bins, cols), 1)
    first = side_ref[0] == 0

    def finish(t, packed):
        value = joined_ref[t] / total_ref[t]
        joined_ref[t] = value
        shift = halo * t + jnp.where(first, halo, 0)
        shift = jnp.where(shift >= cols, shift - cols, shift)
        moved = pltpu.roll(value, shift, 1)
        here = (place >= halo * t) & (place < halo * t + halo)
        return jnp.where(here, moved, packed)

    packed_ref[...] = lax.fori_loop(0, tiles, finish, jnp.zeros((bins, cols), jnp.float32), unroll=4)


def refine_kernel(layers, joined_ref, packed_ref, kernel_ref, out_ref,
                  edge_rows, edge_cols, cur_ref, even_ref, odd_ref, weights_ref, send_sems, recv_sems):
    tiles, bins, cols = joined_ref.shape
    halo = layers
    row, col = lax.axis_index("row"), lax.axis_index("col")
    has_up = row > 0
    has_down = row < lax.axis_size("row") - 1
    other = 1 - col
    barrier = pltpu.get_barrier_semaphore()

    def greet(device):
        pl.semaphore_signal(barrier, inc=1, device_id=device, device_id_type=pl.DeviceIdType.MESH)

    greet((row, other))

    @pl.when(has_up)
    def _():
        greet((row - 1, col))
        greet((row - 1, other))

    @pl.when(has_down)
    def _():
        greet((row + 1, col))
        greet((row + 1, other))

    pl.semaphore_wait(barrier, 1 + 2 * has_up.astype(jnp.int32) + 2 * has_down.astype(jnp.int32))

    def copy(source, target, slot, device):
        return pltpu.make_async_remote_copy(
            src_ref=source, dst_ref=target, send_sem=send_sems.at[slot], recv_sem=recv_sems.at[slot],
            device_id=device, device_id_type=pl.DeviceIdType.MESH)

    leading = joined_ref.at[0:halo]
    trailing = joined_ref.at[tiles - halo : tiles]
    to_side = copy(packed_ref, edge_cols.at[0], 2, (row, other))
    to_down = copy(trailing, edge_rows.at[0], 0, (row + 1, col))
    to_down_side = copy(packed_ref, edge_cols.at[1], 3, (row + 1, other))
    to_up = copy(leading, edge_rows.at[1], 1, (row - 1, col))
    to_up_side = copy(packed_ref, edge_cols.at[2], 4, (row - 1, other))
    to_side.start()

    @pl.when(has_up)
    def _():
        to_up.start()
        to_up_side.start()

    @pl.when(has_down)
    def _():
        to_down.start()
        to_down_side.start()

    lane = lax.broadcasted_iota(jnp.int32, (bins, cols), 1)
    first = col == 0
    low = jnp.where(first, 0, cols - halo)
    in_edge = (lane >= low) & (lane < low + halo)

    def silu(v):
        half = 0.5 * v
        return (half + half * jnp.tanh(half)).astype(jnp.bfloat16)

    def unpack(tile, at):
        shift = jnp.where(first, 0, cols - halo) - halo * at
        shift = jnp.where(shift < 0, shift + cols, shift)
        return jnp.where(in_edge, pltpu.roll(tile, shift, 1), 0.0)

    def put_main(r, main):
        at = pl.multiple_of(r * bins, bins)
        cur_ref[pl.ds(at, bins), 0:cols] = main
        even_ref[pl.ds(at, bins), 0:cols] = silu(main)

    def put_side(r, side):
        at = pl.multiple_of(r * bins, bins)
        cur_ref[pl.ds(at, bins), cols : 2 * cols] = side
        even_ref[pl.ds(at, bins), cols : 2 * cols] = silu(side)

    def put(r, main, side):
        put_main(r, main)
        put_side(r, side)

    def fill_main(t, carry):
        put_main(t + halo, joined_ref[t])
        return carry

    def fill_side(t, carry):
        put_side(t + halo, unpack(edge_cols[0], t))
        return carry

    lax.fori_loop(0, tiles, fill_main, 0, unroll=4)
    group_in = lax.broadcasted_iota(jnp.int32, (bins, bins), 0) // (bins // GROUPS)
    group_out = lax.broadcasted_iota(jnp.int32, (bins, bins), 1) // (bins // GROUPS)
    empty = jnp.zeros((bins, bins), jnp.bfloat16)

    def widen(layer, carry):
        for dc in range(3):
            blocks = []
            for dr in range(3):
                own = kernel_ref[layer, dr, dc].astype(jnp.float32)
                full = jnp.where(group_in == group_out, jnp.concatenate([own] * GROUPS, axis=0), 0.0)
                blocks.append(full.T.astype(jnp.bfloat16))
            weights_ref[layer, dc * bins : (dc + 1) * bins, :] = jnp.concatenate(blocks + [empty], axis=1)
            weights_ref[layer, (3 + dc) * bins : (4 + dc) * bins, :] = jnp.concatenate([empty] + blocks, axis=1)
        return carry

    lax.fori_loop(0, layers, widen, 0)
    to_side.wait_recv()
    lax.fori_loop(0, tiles, fill_side, 0, unroll=4)
    nothing = jnp.zeros((bins, cols), jnp.float32)
    outer = jnp.zeros((bins, 2 * cols), jnp.bfloat16)
    odd_ref[0:bins, :] = outer
    odd_ref[(tiles + 2 * halo - 1) * bins : (tiles + 2 * halo) * bins, :] = outer

    @pl.when(has_up)
    def _():
        to_down.wait_recv()
        to_down_side.wait_recv()
        for i in range(halo):
            put(i, edge_rows[0, i], unpack(edge_cols[1], tiles - halo + i))

    @pl.when(jnp.logical_not(has_up))
    def _():
        for i in range(halo):
            put(i, nothing, nothing)

    @pl.when(has_down)
    def _():
        to_up.wait_recv()
        to_up_side.wait_recv()
        for i in range(halo):
            put(tiles + halo + i, edge_rows[1, i], unpack(edge_cols[2], i))

    @pl.when(jnp.logical_not(has_down))
    def _():
        for i in range(halo):
            put(tiles + halo + i, nothing, nothing)

    wide_lane = lax.broadcasted_iota(jnp.int32, (bins, 2 * cols), 1)
    wide_low = jnp.where(first, 0, 2 * cols - halo)
    col_inside = (wide_lane < cols) | ((wide_lane >= jnp.where(first, cols, 2 * cols - halo))
                                       & (wide_lane < jnp.where(first, cols + halo, 2 * cols)))
    top = jnp.where(has_up, 0, halo)
    bottom = jnp.where(has_down, tiles + 2 * halo, tiles + halo)
    pair = 2
    batch = 2
    stride = pair * batch
    for layer in range(layers):
        now_ref, later_ref = (even_ref, odd_ref) if layer % 2 == 0 else (odd_ref, even_ref)
        last = layer == layers - 1
        begin = halo if last else 1
        end = tiles + halo if last else tiles + 2 * halo - 1

        def rows(step, carry):
            base = begin + step * stride
            values = []
            for one in range(batch):
                at = (base + one * pair) * bins
                window = now_ref[pl.ds(pl.multiple_of(at - bins, bins), (pair + 2) * bins), :]
                parts = jnp.dot(weights_ref[layer], window, preferred_element_type=jnp.float32)
                for j in range(pair):
                    part = parts[3 * bins * j : 3 * bins * (j + 1)]
                    response = (pltpu.roll(part[0:bins], 1, 1) + part[bins : 2 * bins]
                                + pltpu.roll(part[2 * bins : 3 * bins], 2 * cols - 1, 1))
                    spot = pl.ds(pl.multiple_of(at + j * bins, bins), bins)
                    r = base + one * pair + j
                    if last:
                        values.append((r, spot, cur_ref[spot, 0:cols] + response[:, 0:cols]))
                    else:
                        values.append((r, spot, cur_ref[spot, :] + response))
            for r, spot, value in values:
                if last:
                    out_ref[r - halo] = value
                else:
                    cur_ref[spot, :] = value
                    keep = col_inside & (r >= top) & (r < bottom)
                    later_ref[spot, :] = silu(jnp.where(keep, value, 0.0))
            return carry

        lax.fori_loop(0, (end - begin) // stride, rows, 0)

    to_side.wait_send()

    @pl.when(has_up)
    def _():
        to_up.wait_send()
        to_up_side.wait_send()

    @pl.when(has_down)
    def _():
        to_down.wait_send()
        to_down_side.wait_send()


def on_device(
    tsdf_prior, prior_weight, depth_maps, confidence, frustum_tiles, pixel_index, conv_weights
):
    tiles, bins, cols = tsdf_prior.shape
    owners, cap = frustum_tiles.shape[1:]
    layers = conv_weights.shape[0]
    pixels = depth_maps.shape[1]
    f32 = jnp.float32
    got, ids = pl.pallas_call(
        sample_kernel,
        out_shape=(jax.ShapeDtypeStruct((owners, 3 * cap, cols), f32),
                   jax.ShapeDtypeStruct((owners, cap, cols), jnp.int32)),
        in_specs=vmem_specs(4),
        out_specs=tuple(vmem_specs(2)),
        scratch_shapes=[
            VMEM((3 * LANES, pixels // LANES), jnp.bfloat16),
            VMEM((owners, 3 * cap, cols), f32),
            pltpu.SemaphoreType.DMA((owners - 1,)),
            pltpu.SemaphoreType.DMA((owners - 1,)),
        ],
        compiler_params=pltpu.CompilerParams(collective_id=1, has_side_effects=True, vmem_limit_bytes=20 << 20),
        name="sample",
    )(pixel_index[0], depth_maps.reshape(-1, LANES), confidence.reshape(-1, LANES), frustum_tiles[0].T)
    side = lax.axis_index("col").astype(jnp.int32).reshape(1)
    field = jax.ShapeDtypeStruct((tiles, bins, cols), f32)
    joined, new_weight, packed = pl.pallas_call(
        functools.partial(join_kernel, layers),
        out_shape=(field, field, jax.ShapeDtypeStruct((bins, cols), f32)),
        in_specs=[pl.BlockSpec(memory_space=pltpu.SMEM)] * 2 + vmem_specs(3),
        out_specs=tuple(vmem_specs(3)),
        compiler_params=pltpu.CompilerParams(vmem_limit_bytes=20 << 20),
        name="join",
    )(ids, side, got, tsdf_prior, prior_weight)
    total_rows = tiles + 2 * layers
    refined = pl.pallas_call(
        functools.partial(refine_kernel, layers),
        out_shape=field,
        in_specs=vmem_specs(3),
        out_specs=pl.BlockSpec(memory_space=VMEM),
        scratch_shapes=[
            VMEM((2, layers, bins, cols), f32),
            VMEM((3, bins, cols), f32),
            VMEM((total_rows * bins, 2 * cols), f32),
            VMEM((total_rows * bins, 2 * cols), jnp.bfloat16),
            VMEM((total_rows * bins, 2 * cols), jnp.bfloat16),
            VMEM((layers, 6 * bins, 4 * bins), jnp.bfloat16),
            pltpu.SemaphoreType.DMA((5,)),
            pltpu.SemaphoreType.DMA((5,)),
        ],
        compiler_params=pltpu.CompilerParams(collective_id=0, has_side_effects=True, vmem_limit_bytes=20 << 20),
        name="refine",
    )(joined, packed, conv_weights.transpose(0, 3, 4, 2, 1))
    return (refined, new_weight)


def solution(mesh):
    placed = (
        P("row", None, "col"),
        P("row", None, "col"),
        P("row", None),
        P("row", None),
        P(("row", "col"), None, None),
        P(("row", "col"), None, None, None),
        P(),
    )
    return jax.shard_map(
        on_device,
        mesh=mesh,
        in_specs=placed,
        out_specs=(P("row", None, "col"), P("row", None, "col")),
        check_vma=False,
    )
```

profile of v0, /device:TPU:11, one launch (start us, length us, event | category | flops | bytes accessed | tf_op | source)
XLA Modules:
  0.0 47.8 jit_solution(16955748770475071777)
XLA Ops:
  0.6 0.0 copy-start
  0.6 0.0 copy-start.2
  0.7 1.1 %copy-done.2 = f32[1,131072]{1,0:T(1,128)S(1)} copy-done((f32[1,131072]{1,0:T(1,128)S(1)}, f32[1,131072]{1,0:T(1,128)}, u32[]{:S(2)}) %copy-start.2) | copy-done | bytes 524312
  1.8 0.0 copy-start.3
  1.8 1.0 %copy-done.3 = f32[1,131072]{1,0:T(1,128)S(1)} copy-done((f32[1,131072]{1,0:T(1,128)S(1)}, f32[1,131072]{1,0:T(1,128)}, u32[]{:S(2)}) %copy-start.3) | copy-done | bytes 524312
  2.8 0.0 copy-start.5
  2.8 0.8 %copy-done.5 = s32[1,32,2,128]{3,2,1,0:T(2,128)S(1)} copy-done((s32[1,32,2,128]{3,2,1,0:T(2,128)S(1)}, s32[1,32,2,128]{3,2,1,0:T(2,128)}, u32[]{:S(2)}) %copy-start.5) | copy-done | bytes 32792
  3.6 0.0 copy-start.6
  3.6 0.7 %copy-done.6 = s32[1,32,2]{1,2,0:T(2,128)S(1)} copy-done((s32[1,32,2]{1,2,0:T(2,128)S(1)}, s32[1,32,2]{1,2,0:T(2,128)}, u32[]{:S(2)}) %copy-start.6) | copy-done | bytes 280
  4.3 16.5 %sample.1 = (f32[32,6,128]{2,1,0:T(8,128)S(1)}, s32[32,2,128]{2,1,0:T(2,128)S(1)}) custom-call(s32[32,2,128]{2,1,0:T(2,128)S(1)} %bitcast.11, f32[1024,128]{1,0:T(8,128)S(1)} %bitcast.8, f32[1024,128]{1,0:T(8,128)S(1)} %bitcast.9, s32[2,32]{1,0:T(2,128)S(1)} %bitcast.12), custom_call_target="tpu_custom_call" | custom-call | tf_op jit(solution)/shard_map/sample/pallas_call | solution.py:361
  20.8 0.0 copy-done
  20.8 0.0 copy-start.1
  20.8 1.2 %copy-done.1 = f32[32,64,128]{2,1,0:T(8,128)S(1)} copy-done((f32[32,64,128]{2,1,0:T(8,128)S(1)}, f32[32,64,128]{2,1,0:T(8,128)}, u32[]{:S(2)}) %copy-start.1) | copy-done | bytes 1048600
  22.0 0.0 copy-start.4
  22.0 4.4 %join.1 = (f32[32,64,128]{2,1,0:T(8,128)S(1)}, f32[32,64,128]{2,1,0:T(8,128)}, f32[64,128]{1,0:T(8,128)S(1)}) custom-call(s32[32,2,128]{2,1,0:T(2,128)S(1)} %get-tuple-element.7.ids_ref, s32[1]{0:T(128)} %bitcast.5.side_ref, f32[32,6,128]{2,1,0:T(8,128)S(1)} %get-tuple-element.8.got_ref, f32[32,64,128]{2,1,0:T(8,128)S(1)} %copy-done, ...), custom_call_target="tpu_custom_call" | custom-call | tf_op jit(solution)/shard_map/join/pallas_call | solution.py:378
  26.5 0.0 copy-done.4
  26.5 20.4 %refine.1 = f32[32,64,128]{2,1,0:T(8,128)S(1)} custom-call(f32[32,64,128]{2,1,0:T(8,128)S(1)} %get-tuple-element.9.joined_ref, f32[64,128]{1,0:T(8,128)S(1)} %get-tuple-element.10.packed_ref, bf16[3,3,3,16,64]{4,3,2,1,0:T(8,128)(2,1)S(1)} %bitcast.10), custom_call_target="tpu_custom_call" | custom-call | tf_op jit(solution)/shard_map/refine/pallas_call | solution.py:387
  46.9 1.0 %copy.10 = f32[32,64,128]{2,1,0:T(8,128)} copy(f32[32,64,128]{2,1,0:T(8,128)S(1)} %refine.1) | data formatting | bytes 2097152
Async XLA Ops:
  0.6 20.2 %copy-start = (f32[32,64,128]{2,1,0:T(8,128)S(1)}, f32[32,64,128]{2,1,0:T(8,128)}, u32[]{:S(2)}) copy-start(f32[32,64,128]{2,1,0:T(8,128)} %prior_ref.1) | copy-start | bytes 3145732
  0.6 1.1 %copy-start.2 = (f32[1,131072]{1,0:T(1,128)S(1)}, f32[1,131072]{1,0:T(1,128)}, u32[]{:S(2)}) copy-start(f32[1,131072]{1,0:T(1,128)} %param.9) | copy-start | bytes 1572868
  1.8 1.0 %copy-start.3 = (f32[1,131072]{1,0:T(1,128)S(1)}, f32[1,131072]{1,0:T(1,128)}, u32[]{:S(2)}) copy-start(f32[1,131072]{1,0:T(1,128)} %param.10) | copy-start | bytes 1572868
  2.8 0.8 %copy-start.5 = (s32[1,32,2,128]{3,2,1,0:T(2,128)S(1)}, s32[1,32,2,128]{3,2,1,0:T(2,128)}, u32[]{:S(2)}) copy-start(s32[1,32,2,128]{3,2,1,0:T(2,128)} %param.12) | copy-start | bytes 98308
  3.6 0.7 %copy-start.6 = (s32[1,32,2]{1,2,0:T(2,128)S(1)}, s32[1,32,2]{1,2,0:T(2,128)}, u32[]{:S(2)}) copy-start(s32[1,32,2]{1,2,0:T(2,128)} %param.11) | copy-start | bytes 772
  20.8 1.2 %copy-start.1 = (f32[32,64,128]{2,1,0:T(8,128)S(1)}, f32[32,64,128]{2,1,0:T(8,128)}, u32[]{:S(2)}) copy-start(f32[32,64,128]{2,1,0:T(8,128)} %weight_ref.1) | copy-start | bytes 3145732
  22.0 4.4 %copy-start.4 = (bf16[3,64,16,3,3]{1,2,4,3,0:T(8,128)(2,1)S(1)}, bf16[3,64,16,3,3]{1,2,4,3,0:T(8,128)(2,1)}, u32[]{:S(2)}) copy-start(bf16[3,64,16,3,3]{1,2,4,3,0:T(8,128)(2,1)} %param.13) | copy-start | bytes 165892
where the time goes:
time: 48.1 us; the launch traced here: 47.8 us
  Pallas kernels  41.3 us (86%)
  local copies, waits for them, and re-layouts  5.8 us (12%)
  between operations  0.69 us (1%)
    pallas_call x1, Pallas kernels, on_device(): pl.pallas_call(functools.partial(refine_kernel, layers), out_shape=field,...  20.4 us
    pallas_call x1, Pallas kernels, on_device(): pl.pallas_call(sample_kernel, out_shape=(jax.ShapeDtypeStruct((owners, 3...  16.5 us
    unnamed x15, local copies, waits for them, and re-layouts  5.8 us
    pallas_call x1, Pallas kernels, on_device(): pl.pallas_call(functools.partial(join_kernel, layers), out_shape=(field,...  4.42 us

commit v1 on v0

--- a/solution.py
+++ b/solution.py
@@ -11,105 +11,193 @@
 TRUNC = 4
 LANES = 128
 VMEM = pltpu.VMEM
+SUB = 8
+UNROLL = 256
+DEPTH_SCALE = 1023.0
+CONF_SCALE = 13000.0
 
 
 def vmem_specs(count):
     return [pl.BlockSpec(memory_space=VMEM)] * count
 
 
-def sample_kernel(places_ref, depth_ref, conf_ref, want_ref, got_ref, ids_ref, table_ref, staged_ref,
-                  send_sems, recv_sems):
-    owners, cap, _ = places_ref.shape
-    depth_rows = depth_ref.shape[0]
+def sample_kernel(depth_hbm, conf_hbm, index_hbm, want_hbm, got_ref, ids_ref, small_ref,
+                  depth_ref, conf_ref, index_ref, want_ref, table_ref, staged_ref, tiles_ref,
+                  in_sems, send_sems, recv_sems, id_send_sems, id_recv_sems):
+    owners = got_ref.shape[0]
+    cap, own_width = want_hbm.shape
+    table_rows = table_ref.shape[0]
     split = lax.axis_size("col")
-    me = lax.axis_index("row") * split + lax.axis_index("col")
+    my_row, my_col = lax.axis_index("row"), lax.axis_index("col")
+    me = my_row * split + my_col
+    chips = owners // split
+    per_pass = 2 * SUB
+    chips_per_pass = per_pass // (split * cap)
+    passes = owners * cap // per_pass
     barrier = pltpu.get_barrier_semaphore()
 
-    def wrapped(place):
-        return jnp.where(place >= owners, place - owners, place)
-
-    def coordinates(place):
+    loads = [pltpu.make_async_copy(src, dst, in_sems.at[i]) for i, (src, dst) in enumerate(
+        ((depth_hbm, depth_ref), (conf_hbm, conf_ref), (index_hbm, index_ref), (want_hbm, want_ref)))]
+    for load in loads:
+        load.start()
+
+    def device(place):
         return (place // split, place % split)
 
+    def peer(k):
+        return (me + 1 + k) % owners
+
     def greet(k, carry):
-        pl.semaphore_signal(barrier, inc=1, device_id=coordinates(wrapped(me + 1 + k)),
-                            device_id_type=pl.DeviceIdType.MESH)
+        pl.semaphore_signal(barrier, inc=1, device_id=device(peer(k)), device_id_type=pl.DeviceIdType.MESH)
         return carry
 
     lax.fori_loop(0, owners - 1, greet, 0)
-    for at in range(0, depth_rows, LANES):
-        block = depth_ref[at : at + LANES, :].T
-        high = block.astype(jnp.bfloat16)
-        table_ref[0:LANES, at : at + LANES] = high
-        table_ref[LANES : 2 * LANES, at : at + LANES] = (block - high.astype(jnp.float32)).astype(jnp.bfloat16)
-        table_ref[2 * LANES : 3 * LANES, at : at + LANES] = conf_ref[at : at + LANES, :].T.astype(jnp.bfloat16)
-    want = want_ref[...].astype(jnp.float32)
-    listed_by = lax.broadcasted_iota(jnp.int32, want.shape, 1)
-    wide = cap * LANES
-
-    def compute(k):
-        owner = wrapped(me + 1 + k)
-        listed = places_ref[owner]
-        index = jnp.concatenate([listed[s : s + 1, :] for s in range(cap)], axis=1)
-        row = index // LANES
-        lane = index % LANES
-        hot = (lax.broadcasted_iota(jnp.int32, (depth_rows, wide), 0) == row)
-        hot = hot.astype(jnp.float32).astype(jnp.bfloat16)
-        found = jnp.dot(table_ref[...], hot, preferred_element_type=jnp.float32)
-        chosen = lax.broadcasted_iota(jnp.int32, (LANES, wide), 0) == lane
-        results = []
-        for value in (found[0:LANES] + found[LANES : 2 * LANES], found[2 * LANES : 3 * LANES]):
-            value = jnp.sum(jnp.where(chosen, value, 0.0), axis=0, keepdims=True)
-            results += [value[:, s * LANES : (s + 1) * LANES] for s in range(cap)]
-        tile = jnp.sum(jnp.where(listed_by == owner, want, 0.0), axis=1, keepdims=True)
-        results.append(jnp.broadcast_to(tile, (cap, LANES)))
-        return owner, jnp.concatenate(results, axis=0)
-
-    def copy(k):
-        owner = wrapped(me + 1 + k)
+    for load in loads:
+        load.wait()
+    width = tiles_ref.shape[1]
+    tiles = want_ref[...]
+    if own_width < width:
+        tiles = jnp.concatenate([tiles, jnp.full((cap, width - own_width), -1, jnp.int32)], axis=1)
+    tiles_ref[...] = tiles
+
+    def pack(i, carry):
+        spot = pl.ds(pl.multiple_of(i * 64, 64), 64)
+        high = (depth_ref[spot, :] * DEPTH_SCALE + 0.5).astype(jnp.int32) - 32768
+        low = (conf_ref[spot, :] * CONF_SCALE + 0.5).astype(jnp.int32)
+        table_ref[spot, :] = high * 65536 + low
+        return carry
+
+    lax.fori_loop(0, table_rows // 64, pack, 0)
+    nothing = jnp.zeros((2, LANES), jnp.int32)
+    staged_ref[1, 0:2, :] = nothing
+    staged_ref[chips, 6:8, :] = nothing
+    pl.semaphore_wait(barrier, owners - 1)
+
+    def id_copy(place, sender):
         return pltpu.make_async_remote_copy(
-            src_ref=staged_ref.at[owner], dst_ref=got_ref.at[me],
-            send_sem=send_sems.at[k], recv_sem=recv_sems.at[k],
-            device_id=coordinates(owner), device_id_type=pl.DeviceIdType.MESH)
-
-    def arrival(k):
-        sender = wrapped(me + owners - 1 - k)
+            src_ref=tiles_ref, dst_ref=ids_ref.at[sender], send_sem=id_send_sems.at[place],
+            recv_sem=id_recv_sems.at[sender], device_id=device(place), device_id_type=pl.DeviceIdType.MESH)
+
+    def send_ids(k, carry):
+        id_copy(peer(k), me).start()
+        return carry
+
+    lax.fori_loop(0, owners - 1, send_ids, 0)
+    ids_ref[me] = tiles
+
+    def copy(chip, core, sender):
         return pltpu.make_async_remote_copy(
-            src_ref=staged_ref.at[sender], dst_ref=got_ref.at[sender],
-            send_sem=send_sems.at[k], recv_sem=recv_sems.at[k],
-            device_id=coordinates(sender), device_id_type=pl.DeviceIdType.MESH)
-
-    def stage(k):
-        pairs = [compute(k), compute(k + 1)]
-        for owner, value in pairs:
-            staged_ref[owner] = value
-
-    stage(0)
-    pl.semaphore_wait(barrier, owners - 1)
-
-    def step(p, carry):
-        copy(2 * p - 2).start()
-        copy(2 * p - 1).start()
-        stage(2 * p)
-        return carry
-
-    lax.fori_loop(1, owners // 2, step, 0)
-    copy(owners - 2).start()
-    got_ref[me] = staged_ref[me]
+            src_ref=staged_ref.at[chip + 1], dst_ref=got_ref.at[sender], send_sem=send_sems.at[chip * split + core],
+            recv_sem=recv_sems.at[sender], device_id=(chip, core), device_id_type=pl.DeviceIdType.MESH)
+
+    def send(chip):
+        @pl.when(chip != my_row)
+        def _():
+            for core in range(split):
+                copy(chip, core, me).start()
+
+        @pl.when(chip == my_row)
+        def _():
+            copy(chip, 1 - my_col, me).start()
+            got_ref[me] = staged_ref[chip + 1]
+
+    my_pass = my_row // chips_per_pass
+
+    def one_pass(k, carry):
+        p = (my_pass + 1 + k) % passes
+        lanes, rows = [], []
+        for half in range(2):
+            index = index_ref[pl.ds(pl.multiple_of(p * per_pass + half * SUB, SUB), SUB), :]
+            lanes.append(jnp.bitwise_and(index, LANES - 1))
+            rows.append(jnp.right_shift(index, 7))
+
+        def block(b, found):
+            found = list(found)
+            base = b * UNROLL
+            left = [row - base for row in rows]
+            for u in range(UNROLL):
+                line = jnp.broadcast_to(table_ref[pl.ds(base + u, 1), :], (SUB, LANES))
+                for half in range(2):
+                    here = jnp.take_along_axis(line, lanes[half], axis=1)
+                    found[half] = jnp.where(left[half] == u, here, found[half])
+            return tuple(found)
+
+        start = (jnp.zeros((SUB, LANES), jnp.int32),) * 2
+        found = lax.fori_loop(0, table_rows // UNROLL, block, start)
+        first = p * chips_per_pass
+        for i in range(chips_per_pass):
+            own = found[i // 2][4 * (i % 2) : 4 * (i % 2) + 4]
+            chip = first + i
+            staged_ref[chip + 1, 2:6, :] = own
+            staged_ref[chip + 2, 0:1, :] = own[1:2]
+            staged_ref[chip + 2, 1:2, :] = own[3:4]
+            staged_ref[chip, 6:7, :] = own[0:1]
+            staged_ref[chip, 7:8, :] = own[2:3]
+        final = k == passes - 1
+
+        @pl.when((k >= 1) & (p >= 1))
+        def _():
+            send(first - 1)
+            send(first)
+
+        @pl.when(p == 0)
+        def _():
+            send(0)
+
+        for i in range(1, chips_per_pass - 1):
+            send(first + i)
+
+        @pl.when(p == passes - 1)
+        def _():
+            send(chips - 1)
+
+        @pl.when((k == passes - 1) & (p < passes - 1))
+        def _():
+            send(first + chips_per_pass - 1)
+            send(first + chips_per_pass)
+
+        return carry
+
+    lax.fori_loop(0, passes, one_pass, 0)
+
+    def drain_ids(k, carry):
+        place = peer(k)
+        id_copy(place, me).wait_send()
+        id_copy(place, place).wait_recv()
+        return carry
+
+    lax.fori_loop(0, owners - 1, drain_ids, 0)
+    lane = lax.broadcasted_iota(jnp.int32, (SUB, LANES), 1)
+    other = my_row * split + 1 - my_col
+    spots = (me, other, me - split, other - split, me + split, other + split)
+    spot = jnp.zeros((SUB, LANES), jnp.int32)
+    for j, place in enumerate(spots):
+        spot = jnp.where(lane == j, jnp.minimum(jnp.maximum(place, 0), owners - 1), spot)
+    flat = []
+    for q in range(0, owners, SUB // cap):
+        part = jnp.concatenate([ids_ref[q + i] for i in range(SUB // cap)], axis=0)
+        flat.append(jnp.take_along_axis(part, spot, axis=1))
+    wanted = jnp.concatenate(flat, axis=0).astype(jnp.float32)
+    for at in range(0, owners * cap, LANES):
+        piece = wanted[at : at + LANES]
+        if piece.shape[0] < LANES:
+            piece = jnp.concatenate([piece, jnp.zeros((LANES - piece.shape[0], LANES), jnp.float32)], axis=0)
+        small_ref[:, at : at + LANES] = piece.T[0:SUB].astype(jnp.int32)
 
     def drain(k, carry):
-        copy(k).wait_send()
-        arrival(k).wait_recv()
+        place = peer(k)
+        copy(place // split, place % split, me).wait_send()
+        copy(place // split, place % split, place).wait_recv()
         return carry
 
     lax.fori_loop(0, owners - 1, drain, 0)
-    ids_ref[...] = got_ref[:, 2 * cap : 3 * cap, :].astype(jnp.int32)
 
 
 def join_kernel(halo, ids_ref, side_ref, got_ref, prior_ref, weight_ref, joined_ref, total_ref, packed_ref):
     tiles, bins, cols = prior_ref.shape
-    readers, rows, _ = got_ref.shape
-    cap = rows // 3
+    readers = got_ref.shape[0]
+    cap = 2
+    side = side_ref[0]
 
     def begin(t, carry):
         weight = weight_ref[t]
@@ -127,10 +215,11 @@
         for one in range(batch):
             reader = step * batch + one
             for s in range(cap):
-                listed = ids_ref[reader, s, 0]
+                listed = ids_ref[0, reader * cap + s]
                 tile = jnp.maximum(listed, 0)
-                height = got_ref[reader, s : s + 1, :]
-                sure = got_ref[reader, cap + s : cap + s + 1, :]
+                word = got_ref[reader, pl.ds(2 + 2 * side + s, 1), :]
+                height = (jnp.right_shift(word, 16) + 32768).astype(jnp.float32) * (1.0 / DEPTH_SCALE)
+                sure = jnp.bitwise_and(word, 65535).astype(jnp.float32) * (1.0 / CONF_SCALE)
                 sure = jnp.where(listed >= 0, sure, 0.0)
                 scaled = (height - levels) * (1.0 / TRUNC)
                 signed = jnp.clip(scaled, -1.0, 1.0)
@@ -358,21 +447,34 @@
     layers = conv_weights.shape[0]
     pixels = depth_maps.shape[1]
     f32 = jnp.float32
-    got, ids = pl.pallas_call(
+    width = -(-owners // LANES) * LANES
+    small = -(-owners * cap // LANES) * LANES
+    i32 = jnp.int32
+    hbm = pl.BlockSpec(memory_space=pltpu.HBM)
+    got, _, ids = pl.pallas_call(
         sample_kernel,
-        out_shape=(jax.ShapeDtypeStruct((owners, 3 * cap, cols), f32),
-                   jax.ShapeDtypeStruct((owners, cap, cols), jnp.int32)),
-        in_specs=vmem_specs(4),
-        out_specs=tuple(vmem_specs(2)),
+        out_shape=(jax.ShapeDtypeStruct((owners, SUB, LANES), i32),
+                   jax.ShapeDtypeStruct((owners, cap, width), i32),
+                   jax.ShapeDtypeStruct((SUB, small), i32)),
+        in_specs=[hbm] * 4,
+        out_specs=tuple(vmem_specs(3)),
         scratch_shapes=[
-            VMEM((3 * LANES, pixels // LANES), jnp.bfloat16),
-            VMEM((owners, 3 * cap, cols), f32),
-            pltpu.SemaphoreType.DMA((owners - 1,)),
-            pltpu.SemaphoreType.DMA((owners - 1,)),
+            VMEM((pixels // LANES, LANES), f32),
+            VMEM((pixels // LANES, LANES), f32),
+            VMEM((owners * cap, LANES), i32),
+            VMEM((cap, owners), i32),
+            VMEM((pixels // LANES, LANES), i32),
+            VMEM((owners // 2 + 2, SUB, LANES), i32),
+            VMEM((cap, width), i32),
+            pltpu.SemaphoreType.DMA((4,)),
+            pltpu.SemaphoreType.DMA((owners,)),
+            pltpu.SemaphoreType.DMA((owners,)),
+            pltpu.SemaphoreType.DMA((owners,)),
+            pltpu.SemaphoreType.DMA((owners,)),
         ],
         compiler_params=pltpu.CompilerParams(collective_id=1, has_side_effects=True, vmem_limit_bytes=20 << 20),
         name="sample",
-    )(pixel_index[0], depth_maps.reshape(-1, LANES), confidence.reshape(-1, LANES), frustum_tiles[0].T)
+    )(depth_maps.reshape(-1, LANES), confidence.reshape(-1, LANES), pixel_index.reshape(-1, LANES), frustum_tiles[0].T)
     side = lax.axis_index("col").astype(jnp.int32).reshape(1)
     field = jax.ShapeDtypeStruct((tiles, bins, cols), f32)
     joined, new_weight, packed = pl.pallas_call(

time: 48.1 us -> 51.1 us (1.062)
  Pallas kernels: 41.3 us -> 44.3 us
    pallas_call x1, Pallas kernels: 16.5 us -> 20 us  [on_device(): pl.pallas_call(sample_kernel, out_shape=(jax.ShapeDtypeStruct((owners, SU...]
    pallas_call x1, Pallas kernels: 4.42 us -> 3.88 us  [on_device(): pl.pallas_call(functools.partial(join_kernel, layers), out_shape=(field,...]
where the time goes in v1:
time: 51.1 us; the launch traced here: 50.8 us
  Pallas kernels  44.3 us (87%)
  local copies, waits for them, and re-layouts  5.8 us (11%)
  between operations  0.69 us (1%)
    pallas_call x1, Pallas kernels, on_device(): pl.pallas_call(functools.partial(refine_kernel, layers), out_shape=field,...  20.4 us
    pallas_call x1, Pallas kernels, on_device(): pl.pallas_call(sample_kernel, out_shape=(jax.ShapeDtypeStruct((owners, SU...  20 us
    unnamed x15, local copies, waits for them, and re-layouts  5.8 us
    pallas_call x1, Pallas kernels, on_device(): pl.pallas_call(functools.partial(join_kernel, layers), out_shape=(field,...  3.88 us

profile of v1, /device:TPU:11, one launch (start us, length us, event | category | flops | bytes accessed | tf_op | source)
XLA Modules:
  0.0 50.8 jit_solution(11118349681876593089)
XLA Ops:
  0.6 0.0 copy-start
  0.6 0.0 copy-start.2
  0.7 1.1 %copy-done.2 = f32[1,131072]{1,0:T(1,128)S(1)} copy-done((f32[1,131072]{1,0:T(1,128)S(1)}, f32[1,131072]{1,0:T(1,128)}, u32[]{:S(2)}) %copy-start.2) | copy-done | bytes 524312
  1.8 0.0 copy-start.3
  1.8 1.0 %copy-done.3 = f32[1,131072]{1,0:T(1,128)S(1)} copy-done((f32[1,131072]{1,0:T(1,128)S(1)}, f32[1,131072]{1,0:T(1,128)}, u32[]{:S(2)}) %copy-start.3) | copy-done | bytes 524312
  2.8 0.0 copy-start.5
  2.8 0.8 %copy-done.5 = s32[1,32,2,128]{3,2,1,0:T(2,128)S(1)} copy-done((s32[1,32,2,128]{3,2,1,0:T(2,128)S(1)}, s32[1,32,2,128]{3,2,1,0:T(2,128)}, u32[]{:S(2)}) %copy-start.5) | copy-done | bytes 32792
  3.6 0.0 copy-start.6
  3.6 0.7 %copy-done.6 = s32[1,32,2]{1,2,0:T(2,128)S(1)} copy-done((s32[1,32,2]{1,2,0:T(2,128)S(1)}, s32[1,32,2]{1,2,0:T(2,128)}, u32[]{:S(2)}) %copy-start.6) | copy-done | bytes 280
  4.3 20.0 %sample.1 = (s32[32,8,128]{2,1,0:T(8,128)S(1)}, s32[32,2,128]{2,1,0:T(2,128)}, s32[8,128]{1,0:T(8,128)S(1)}) custom-call(f32[1024,128]{1,0:T(8,128)S(1)} %bitcast.8, f32[1024,128]{1,0:T(8,128)S(1)} %bitcast.9, s32[64,128]{1,0:T(8,128)S(1)} %bitcast.11, s32[2,32]{1,0:T(2,128)S(1)} %bitcast.12), custom_call_target="tpu_custom_call" | custom-call | tf_op jit(solution)/shard_map/sample/pallas_call | solution.py:454
  24.3 0.0 copy-done
  24.3 0.0 copy-start.1
  24.3 1.2 %copy-done.1 = f32[32,64,128]{2,1,0:T(8,128)S(1)} copy-done((f32[32,64,128]{2,1,0:T(8,128)S(1)}, f32[32,64,128]{2,1,0:T(8,128)}, u32[]{:S(2)}) %copy-start.1) | copy-done | bytes 1048600
  25.5 0.0 copy-start.4
  25.5 3.9 %join.1 = (f32[32,64,128]{2,1,0:T(8,128)S(1)}, f32[32,64,128]{2,1,0:T(8,128)}, f32[64,128]{1,0:T(8,128)S(1)}) custom-call(s32[8,128]{1,0:T(8,128)S(1)} %get-tuple-element.7.ids_ref, s32[1]{0:T(128)} %bitcast.5.side_ref, s32[32,8,128]{2,1,0:T(8,128)S(1)} %get-tuple-element.8.got_ref, f32[32,64,128]{2,1,0:T(8,128)S(1)} %copy-done, f32[32,64,128]{2,1,0:T(8,128)S(1)} %copy-done.1), custom_call_target="tpu_custom_call" | custom-call | tf_op jit(solution)/shard_map/join/pallas_call | solution.py:480
  29.4 0.0 copy-done.4
  29.4 20.4 %refine.1 = f32[32,64,128]{2,1,0:T(8,128)S(1)} custom-call(f32[32,64,128]{2,1,0:T(8,128)S(1)} %get-tuple-element.9.joined_ref, f32[64,128]{1,0:T(8,128)S(1)} %get-tuple-element.10.packed_ref, bf16[3,3,3,16,64]{4,3,2,1,0:T(8,128)(2,1)S(1)} %bitcast.10), custom_call_target="tpu_custom_call" | custom-call | tf_op jit(solution)/shard_map/refine/pallas_call | solution.py:489
  49.8 1.0 %copy.10 = f32[32,64,128]{2,1,0:T(8,128)} copy(f32[32,64,128]{2,1,0:T(8,128)S(1)} %refine.1) | data formatting | bytes 2097152
Async XLA Ops:
  0.6 23.6 %copy-start = (f32[32,64,128]{2,1,0:T(8,128)S(1)}, f32[32,64,128]{2,1,0:T(8,128)}, u32[]{:S(2)}) copy-start(f32[32,64,128]{2,1,0:T(8,128)} %prior_ref.1) | copy-start | bytes 3145732
  0.6 1.1 %copy-start.2 = (f32[1,131072]{1,0:T(1,128)S(1)}, f32[1,131072]{1,0:T(1,128)}, u32[]{:S(2)}) copy-start(f32[1,131072]{1,0:T(1,128)} %param.9) | copy-start | bytes 1572868
  1.8 1.0 %copy-start.3 = (f32[1,131072]{1,0:T(1,128)S(1)}, f32[1,131072]{1,0:T(1,128)}, u32[]{:S(2)}) copy-start(f32[1,131072]{1,0:T(1,128)} %param.10) | copy-start | bytes 1572868
  2.8 0.8 %copy-start.5 = (s32[1,32,2,128]{3,2,1,0:T(2,128)S(1)}, s32[1,32,2,128]{3,2,1,0:T(2,128)}, u32[]{:S(2)}) copy-start(s32[1,32,2,128]{3,2,1,0:T(2,128)} %param.12) | copy-start | bytes 98308
  3.6 0.7 %copy-start.6 = (s32[1,32,2]{1,2,0:T(2,128)S(1)}, s32[1,32,2]{1,2,0:T(2,128)}, u32[]{:S(2)}) copy-start(s32[1,32,2]{1,2,0:T(2,128)} %param.11) | copy-start | bytes 772
  24.3 1.2 %copy-start.1 = (f32[32,64,128]{2,1,0:T(8,128)S(1)}, f32[32,64,128]{2,1,0:T(8,128)}, u32[]{:S(2)}) copy-start(f32[32,64,128]{2,1,0:T(8,128)} %weight_ref.1) | copy-start | bytes 3145732
  25.5 3.9 %copy-start.4 = (bf16[3,64,16,3,3]{1,2,4,3,0:T(8,128)(2,1)S(1)}, bf16[3,64,16,3,3]{1,2,4,3,0:T(8,128)(2,1)}, u32[]{:S(2)}) copy-start(bf16[3,64,16,3,3]{1,2,4,3,0:T(8,128)(2,1)} %param.13) | copy-start | bytes 165892

commit v2 on v0

--- a/solution.py
+++ b/solution.py
@@ -11,14 +11,20 @@
 TRUNC = 4
 LANES = 128
 VMEM = pltpu.VMEM
+UNROLL_ROWS = 4
 
 
 def vmem_specs(count):
     return [pl.BlockSpec(memory_space=VMEM)] * count
 
 
-def sample_kernel(places_ref, depth_ref, conf_ref, want_ref, got_ref, ids_ref, table_ref, staged_ref,
-                  send_sems, recv_sems):
+def sample_kernel(places_hbm, depth_hbm, conf_hbm, want_hbm, got_ref, ids_ref,
+                  places_ref, depth_ref, conf_ref, want_ref, table_ref, staged_ref,
+                  in_sems, send_sems, recv_sems):
+    loads = [pltpu.make_async_copy(src, dst, in_sems.at[i]) for i, (src, dst) in enumerate(
+        ((depth_hbm, depth_ref), (conf_hbm, conf_ref), (places_hbm, places_ref), (want_hbm, want_ref)))]
+    for load in loads:
+        load.start()
     owners, cap, _ = places_ref.shape
     depth_rows = depth_ref.shape[0]
     split = lax.axis_size("col")
@@ -37,6 +43,8 @@
         return carry
 
     lax.fori_loop(0, owners - 1, greet, 0)
+    for load in loads:
+        load.wait()
     for at in range(0, depth_rows, LANES):
         block = depth_ref[at : at + LANES, :].T
         high = block.astype(jnp.bfloat16)
@@ -160,9 +168,11 @@
 
 
 def refine_kernel(layers, joined_ref, packed_ref, kernel_ref, out_ref,
-                  edge_rows, edge_cols, cur_ref, even_ref, odd_ref, weights_ref, send_sems, recv_sems):
+                  edge_rows, edge_cols, cur_ref, even_ref, odd_ref, weights_ref, side_weights_ref,
+                  side_ref, gap_ref, send_sems, recv_sems):
     tiles, bins, cols = joined_ref.shape
     halo = layers
+    total = tiles + 2 * halo
     row, col = lax.axis_index("row"), lax.axis_index("col")
     has_up = row > 0
     has_down = row < lax.axis_size("row") - 1
@@ -194,160 +204,219 @@
     leading = joined_ref.at[0:halo]
     trailing = joined_ref.at[tiles - halo : tiles]
     to_side = copy(packed_ref, edge_cols.at[0], 2, (row, other))
-    to_down = copy(trailing, edge_rows.at[0], 0, (row + 1, col))
-    to_down_side = copy(packed_ref, edge_cols.at[1], 3, (row + 1, other))
-    to_up = copy(leading, edge_rows.at[1], 1, (row - 1, col))
-    to_up_side = copy(packed_ref, edge_cols.at[2], 4, (row - 1, other))
+    to_down = [copy(packed_ref, edge_cols.at[1], 3, (row + 1, other)),
+               copy(packed_ref, edge_cols.at[3], 5, (row + 1, col)),
+               copy(trailing, edge_rows.at[0], 0, (row + 1, col))]
+    to_up = [copy(packed_ref, edge_cols.at[2], 4, (row - 1, other)),
+             copy(packed_ref, edge_cols.at[4], 6, (row - 1, col)),
+             copy(leading, edge_rows.at[1], 1, (row - 1, col))]
     to_side.start()
 
     @pl.when(has_up)
     def _():
-        to_up.start()
-        to_up_side.start()
+        for one in to_up:
+            one.start()
 
     @pl.when(has_down)
     def _():
-        to_down.start()
-        to_down_side.start()
-
+        for one in to_down:
+            one.start()
+
+    first = col == 0
+    near, far = jnp.where(first, cols - 1, 0), jnp.where(first, 0, cols - 1)
+    inward = jnp.where(first, 2, 0)
     lane = lax.broadcasted_iota(jnp.int32, (bins, cols), 1)
-    first = col == 0
-    low = jnp.where(first, 0, cols - halo)
-    in_edge = (lane >= low) & (lane < low + halo)
+    is_near, is_far = lane == near, lane == far
 
     def silu(v):
         half = 0.5 * v
-        return (half + half * jnp.tanh(half)).astype(jnp.bfloat16)
-
-    def unpack(tile, at):
-        shift = jnp.where(first, 0, cols - halo) - halo * at
-        shift = jnp.where(shift < 0, shift + cols, shift)
-        return jnp.where(in_edge, pltpu.roll(tile, shift, 1), 0.0)
-
-    def put_main(r, main):
-        at = pl.multiple_of(r * bins, bins)
-        cur_ref[pl.ds(at, bins), 0:cols] = main
-        even_ref[pl.ds(at, bins), 0:cols] = silu(main)
-
-    def put_side(r, side):
-        at = pl.multiple_of(r * bins, bins)
-        cur_ref[pl.ds(at, bins), cols : 2 * cols] = side
-        even_ref[pl.ds(at, bins), cols : 2 * cols] = silu(side)
-
-    def put(r, main, side):
-        put_main(r, main)
-        put_side(r, side)
-
-    def fill_main(t, carry):
-        put_main(t + halo, joined_ref[t])
-        return carry
-
-    def fill_side(t, carry):
-        put_side(t + halo, unpack(edge_cols[0], t))
-        return carry
-
-    lax.fori_loop(0, tiles, fill_main, 0, unroll=4)
+        return half + half * jnp.tanh(half)
+
+    def put(r, value):
+        spot = pl.ds(pl.multiple_of(r * bins, bins), bins)
+        cur_ref[spot, :] = value
+        even_ref[spot, :] = silu(value).astype(jnp.bfloat16)
+
     group_in = lax.broadcasted_iota(jnp.int32, (bins, bins), 0) // (bins // GROUPS)
     group_out = lax.broadcasted_iota(jnp.int32, (bins, bins), 1) // (bins // GROUPS)
     empty = jnp.zeros((bins, bins), jnp.bfloat16)
 
     def widen(layer, carry):
-        for dc in range(3):
-            blocks = []
-            for dr in range(3):
-                own = kernel_ref[layer, dr, dc].astype(jnp.float32)
-                full = jnp.where(group_in == group_out, jnp.concatenate([own] * GROUPS, axis=0), 0.0)
-                blocks.append(full.T.astype(jnp.bfloat16))
-            weights_ref[layer, dc * bins : (dc + 1) * bins, :] = jnp.concatenate(blocks + [empty], axis=1)
-            weights_ref[layer, (3 + dc) * bins : (4 + dc) * bins, :] = jnp.concatenate([empty] + blocks, axis=1)
+        def dense(dr, dc):
+            own = kernel_ref[layer, dr, dc].astype(jnp.float32)
+            full = jnp.where(group_in == group_out, jnp.concatenate([own] * GROUPS, axis=0), 0.0)
+            return full.T.astype(jnp.bfloat16)
+
+        for at, dc in ((0, 2 - inward), (1, 1), (2, inward)):
+            blocks = [dense(dr, dc) for dr in range(3)]
+            weights_ref[layer, at * bins : (at + 1) * bins, :] = jnp.concatenate(blocks + [empty], axis=1)
+            weights_ref[layer, (3 + at) * bins : (4 + at) * bins, :] = jnp.concatenate([empty] + blocks, axis=1)
+        below = [dense(dr, inward) if dc == 1 else empty for dr in range(3) for dc in range(3)]
+        side_weights_ref[layer, 0:bins, :] = jnp.concatenate(
+            [dense(dr, dc) for dr in range(3) for dc in range(3)], axis=1)
+        side_weights_ref[layer, bins : 2 * bins, :] = jnp.concatenate(below, axis=1)
+        return carry
+
+    def fill(t, carry):
+        put(t + halo, joined_ref[t])
         return carry
 
     lax.fori_loop(0, layers, widen, 0)
+    lax.fori_loop(0, tiles, fill, 0, unroll=4)
+
+    wide = side_ref.shape[1]
+    span = 2 * halo - 1
+    half_lane = [lane + at for at in range(0, wide, cols)]
+    place = [one // span for one in half_lane]
+    spot_in = [one % span for one in half_lane]
+    mine_low, mine_high = jnp.where(first, 0, halo), jnp.where(first, halo - 1, span)
+    mine = [(one >= mine_low) & (one < mine_high) for one in spot_in]
+    mine_col = jnp.where(first, 1, -halo)
+    side_col = jnp.where(first, 1 - halo, 0)
+    shift_in = [one + jnp.where(m, mine_col, side_col) for one, m in zip(spot_in, mine)]
+
+    def collect(own, neighbour, h, offset, low, high):
+        source = (place[h] - offset) * halo + shift_in[h]
+        source = jnp.minimum(jnp.maximum(source, 0), cols - 1)
+        value = jnp.where(mine[h], jnp.take_along_axis(own, source, axis=1),
+                          jnp.take_along_axis(neighbour, source, axis=1))
+        return value, (place[h] >= low) & (place[h] < high)
+
     to_side.wait_recv()
-    lax.fori_loop(0, tiles, fill_side, 0, unroll=4)
+    for h in range(len(place)):
+        value, here = collect(packed_ref[...], edge_cols[0], h, halo, halo, halo + tiles)
+        side_ref[:, h * cols : (h + 1) * cols] = jnp.where(here, value, 0.0)
+    outer = jnp.zeros((bins, cols), jnp.bfloat16)
+    odd_ref[0:bins, :] = outer
+    odd_ref[(total - 1) * bins : total * bins, :] = outer
     nothing = jnp.zeros((bins, cols), jnp.float32)
-    outer = jnp.zeros((bins, 2 * cols), jnp.bfloat16)
-    odd_ref[0:bins, :] = outer
-    odd_ref[(tiles + 2 * halo - 1) * bins : (tiles + 2 * halo) * bins, :] = outer
+
+    def join_side(own, neighbour, offset, low, high):
+        for h in range(len(place)):
+            if low < (h + 1) * cols // span + 1 and high > h * cols // span:
+                value, here = collect(own, neighbour, h, offset, low, high)
+                part = side_ref[:, h * cols : (h + 1) * cols]
+                side_ref[:, h * cols : (h + 1) * cols] = jnp.where(here, value, part)
 
     @pl.when(has_up)
     def _():
-        to_down.wait_recv()
-        to_down_side.wait_recv()
+        for one in to_down:
+            one.wait_recv()
+        join_side(edge_cols[3], edge_cols[1], halo - tiles, 0, halo)
         for i in range(halo):
-            put(i, edge_rows[0, i], unpack(edge_cols[1], tiles - halo + i))
+            put(i, edge_rows[0, i])
 
     @pl.when(jnp.logical_not(has_up))
     def _():
         for i in range(halo):
-            put(i, nothing, nothing)
+            put(i, nothing)
 
     @pl.when(has_down)
     def _():
-        to_up.wait_recv()
-        to_up_side.wait_recv()
+        for one in to_up:
+            one.wait_recv()
+        join_side(edge_cols[4], edge_cols[2], halo + tiles, halo + tiles, total)
         for i in range(halo):
-            put(tiles + halo + i, edge_rows[1, i], unpack(edge_cols[2], i))
+            put(tiles + halo + i, edge_rows[1, i])
 
     @pl.when(jnp.logical_not(has_down))
     def _():
         for i in range(halo):
-            put(tiles + halo + i, nothing, nothing)
-
-    wide_lane = lax.broadcasted_iota(jnp.int32, (bins, 2 * cols), 1)
-    wide_low = jnp.where(first, 0, 2 * cols - halo)
-    col_inside = (wide_lane < cols) | ((wide_lane >= jnp.where(first, cols, 2 * cols - halo))
-                                       & (wide_lane < jnp.where(first, cols + halo, 2 * cols)))
-    top = jnp.where(has_up, 0, halo)
-    bottom = jnp.where(has_down, tiles + 2 * halo, tiles + halo)
+            put(tiles + halo + i, nothing)
+
+    wide_place = lax.broadcasted_iota(jnp.int32, (bins, wide), 1) // span
+    inside = ((wide_place >= jnp.where(has_up, 0, halo))
+              & (wide_place < jnp.where(has_down, total, tiles + halo)))
+    middle = span // 2
+
+    def side_step(layer, carry):
+        now = side_ref[...]
+        active = silu(now)
+        shifted = []
+        for dr in range(-1, 2):
+            for dc in range(-1, 2):
+                offset = (-(span * dr + dc)) % wide
+                moved = active if offset == 0 else pltpu.roll(active, offset, 1)
+                shifted.append(moved.astype(jnp.bfloat16))
+        result = jnp.dot(side_weights_ref[layer], jnp.concatenate(shifted, axis=0),
+                         preferred_element_type=jnp.float32)
+        side_ref[...] = jnp.where(inside, now + result[0:bins], 0.0)
+        gap = nothing
+        for h in range(len(place)):
+            source = lane * span + middle - h * cols
+            ok = (source >= 0) & (source < cols)
+            moved = jnp.take_along_axis(result[bins : 2 * bins, h * cols : (h + 1) * cols],
+                                        jnp.minimum(jnp.maximum(source, 0), cols - 1), axis=1)
+            gap = jnp.where(ok, moved, gap)
+        gap_ref[layer] = gap
+        return carry
+
+    lax.fori_loop(0, layers, side_step, 0)
+    inner_shift, outer_shift = jnp.where(first, cols - 1, 1), jnp.where(first, 1, cols - 1)
     pair = 2
-    batch = 2
-    stride = pair * batch
+    stride = 2 * pair
     for layer in range(layers):
         now_ref, later_ref = (even_ref, odd_ref) if layer % 2 == 0 else (odd_ref, even_ref)
         last = layer == layers - 1
         begin = halo if last else 1
-        end = tiles + halo if last else tiles + 2 * halo - 1
+        end = tiles + halo if last else total - 1
+
+        steps = (end - begin) // stride
+        unroll = max(u for u in range(1, UNROLL_ROWS + 1) if steps % u == 0)
+
+        def store(r, spot, value):
+            if last:
+                out_ref[r - halo] = value
+            else:
+                cur_ref[spot, :] = value
+                later_ref[spot, :] = silu(value).astype(jnp.bfloat16)
 
         def rows(step, carry):
-            base = begin + step * stride
-            values = []
-            for one in range(batch):
-                at = (base + one * pair) * bins
-                window = now_ref[pl.ds(pl.multiple_of(at - bins, bins), (pair + 2) * bins), :]
+            for one in range(unroll):
+                base = begin + step * (stride * unroll) + one * stride
+                at = base * bins
+                span_rows = (pair + 2) * bins
+                window = jnp.concatenate(
+                    [now_ref[pl.ds(pl.multiple_of(at - bins + h * pair * bins, bins), span_rows), :]
+                     for h in range(2)], axis=1)
                 parts = jnp.dot(weights_ref[layer], window, preferred_element_type=jnp.float32)
-                for j in range(pair):
-                    part = parts[3 * bins * j : 3 * bins * (j + 1)]
-                    response = (pltpu.roll(part[0:bins], 1, 1) + part[bins : 2 * bins]
-                                + pltpu.roll(part[2 * bins : 3 * bins], 2 * cols - 1, 1))
-                    spot = pl.ds(pl.multiple_of(at + j * bins, bins), bins)
-                    r = base + one * pair + j
-                    if last:
-                        values.append((r, spot, cur_ref[spot, 0:cols] + response[:, 0:cols]))
-                    else:
-                        values.append((r, spot, cur_ref[spot, :] + response))
-            for r, spot, value in values:
-                if last:
-                    out_ref[r - halo] = value
-                else:
-                    cur_ref[spot, :] = value
-                    keep = col_inside & (r >= top) & (r < bottom)
-                    later_ref[spot, :] = silu(jnp.where(keep, value, 0.0))
+                for h in range(2):
+                    for j in range(pair):
+                        part = parts[3 * bins * j : 3 * bins * (j + 1), h * cols : (h + 1) * cols]
+                        r = base + h * pair + j
+                        shift = near - r
+                        gap = pltpu.roll(gap_ref[layer], jnp.where(shift < 0, shift + cols, shift), 1)
+                        response = (jnp.where(is_far, 0.0, pltpu.roll(part[0:bins], outer_shift, 1))
+                                    + part[bins : 2 * bins]
+                                    + jnp.where(is_near, gap, pltpu.roll(part[2 * bins : 3 * bins], inner_shift, 1)))
+                        spot = pl.ds(pl.multiple_of(r * bins, bins), bins)
+                        value = cur_ref[spot, :] + response
+                        store(r, spot, value)
             return carry
 
-        lax.fori_loop(0, (end - begin) // stride, rows, 0)
+        lax.fori_loop(0, steps // unroll, rows, 0)
+        if not last:
+            blank = jnp.zeros((halo * bins, cols), jnp.bfloat16)
+
+            @pl.when(jnp.logical_not(has_up))
+            def _():
+                later_ref[0 : halo * bins, :] = blank
+
+            @pl.when(jnp.logical_not(has_down))
+            def _():
+                later_ref[(tiles + halo) * bins : total * bins, :] = blank
 
     to_side.wait_send()
 
     @pl.when(has_up)
     def _():
-        to_up.wait_send()
-        to_up_side.wait_send()
+        for one in to_up:
+            one.wait_send()
 
     @pl.when(has_down)
     def _():
-        to_down.wait_send()
-        to_down_side.wait_send()
+        for one in to_down:
+            one.wait_send()
 
 
 def on_device(
@@ -362,17 +431,25 @@
         sample_kernel,
         out_shape=(jax.ShapeDtypeStruct((owners, 3 * cap, cols), f32),
                    jax.ShapeDtypeStruct((owners, cap, cols), jnp.int32)),
-        in_specs=vmem_specs(4),
+        in_specs=[pl.BlockSpec(memory_space=pltpu.HBM)] * 4,
         out_specs=tuple(vmem_specs(2)),
         scratch_shapes=[
+            VMEM((owners, cap, LANES), jnp.int32),
+            VMEM((pixels // LANES, LANES), f32),
+            VMEM((pixels // LANES, LANES), f32),
+            VMEM((cap, owners), jnp.int32),
             VMEM((3 * LANES, pixels // LANES), jnp.bfloat16),
             VMEM((owners, 3 * cap, cols), f32),
+            pltpu.SemaphoreType.DMA((4,)),
             pltpu.SemaphoreType.DMA((owners - 1,)),
             pltpu.SemaphoreType.DMA((owners - 1,)),
         ],
         compiler_params=pltpu.CompilerParams(collective_id=1, has_side_effects=True, vmem_limit_bytes=20 << 20),
+        cost_estimate=pl.CostEstimate(
+            flops=6 * LANES * pixels // LANES * owners * cap * cols, bytes_accessed=8 * pixels, transcendentals=0),
         name="sample",
-    )(pixel_index[0], depth_maps.reshape(-1, LANES), confidence.reshape(-1, LANES), frustum_tiles[0].T)
+    )(*(pltpu.with_memory_space_constraint(one, pltpu.HBM) for one in (
+        pixel_index[0], depth_maps.reshape(-1, LANES), confidence.reshape(-1, LANES), frustum_tiles[0].T)))
     side = lax.axis_index("col").astype(jnp.int32).reshape(1)
     field = jax.ShapeDtypeStruct((tiles, bins, cols), f32)
     joined, new_weight, packed = pl.pallas_call(
@@ -384,6 +461,7 @@
         name="join",
     )(ids, side, got, tsdf_prior, prior_weight)
     total_rows = tiles + 2 * layers
+    wide = -(-total_rows * (2 * layers - 1) // cols) * cols
     refined = pl.pallas_call(
         functools.partial(refine_kernel, layers),
         out_shape=field,
@@ -391,13 +469,16 @@
         out_specs=pl.BlockSpec(memory_space=VMEM),
         scratch_shapes=[
             VMEM((2, layers, bins, cols), f32),
-            VMEM((3, bins, cols), f32),
-            VMEM((total_rows * bins, 2 * cols), f32),
-            VMEM((total_rows * bins, 2 * cols), jnp.bfloat16),
-            VMEM((total_rows * bins, 2 * cols), jnp.bfloat16),
+            VMEM((5, bins, cols), f32),
+            VMEM((total_rows * bins, cols), f32),
+            VMEM((total_rows * bins, cols), jnp.bfloat16),
+            VMEM((total_rows * bins, cols), jnp.bfloat16),
             VMEM((layers, 6 * bins, 4 * bins), jnp.bfloat16),
-            pltpu.SemaphoreType.DMA((5,)),
-            pltpu.SemaphoreType.DMA((5,)),
+            VMEM((layers, 2 * bins, 9 * bins), jnp.bfloat16),
+            VMEM((bins, wide), f32),
+            VMEM((layers, bins, cols), f32),
+            pltpu.SemaphoreType.DMA((7,)),
+            pltpu.SemaphoreType.DMA((7,)),
         ],
         compiler_params=pltpu.CompilerParams(collective_id=0, has_side_effects=True, vmem_limit_bytes=20 << 20),
         name="refine",

time: 48.1 us -> 39.8 us (0.83)
  local copies, waits for them, and re-layouts: 5.8 us -> 0.99 us
  Pallas kernels: 41.3 us -> 38 us
    unnamed x15 -> x7, local copies, waits for them, and re-layouts: 5.8 us -> 0.99 us
    pallas_call x1, Pallas kernels: 20.4 us -> 16.7 us  [on_device(): pl.pallas_call(functools.partial(refine_kernel, layers), out_shape=field,...]
where the time goes in v2:
time: 39.8 us; the launch traced here: 39.6 us
  Pallas kernels  38 us (95%)
  local copies, waits for them, and re-layouts  0.99 us (2%)
  between operations  0.69 us (2%)
    pallas_call x1, Pallas kernels, on_device(): pl.pallas_call(sample_kernel, out_shape=(jax.ShapeDtypeStruct((owners, 3...  16.8 us
    pallas_call x1, Pallas kernels, on_device(): pl.pallas_call(functools.partial(refine_kernel, layers), out_shape=field,...  16.7 us
    pallas_call x1, Pallas kernels, on_device(): pl.pallas_call(functools.partial(join_kernel, layers), out_shape=(field,...  4.45 us
    unnamed x7, local copies, waits for them, and re-layouts  0.99 us

profile of v2, /device:TPU:11, one launch (start us, length us, event | category | flops | bytes accessed | tf_op | source)
XLA Modules:
  0.0 39.6 jit_solution(346716456791594236)
XLA Ops:
  0.6 0.0 copy-start
  0.6 0.0 copy-start.1
  0.7 16.8 %sample.1 = (f32[32,6,128]{2,1,0:T(8,128)S(1)}, s32[32,2,128]{2,1,0:T(2,128)S(1)}) custom-call(s32[32,2,128]{2,1,0:T(2,128)} %bitcast.11, f32[1024,128]{1,0:T(8,128)} %bitcast.9, f32[1024,128]{1,0:T(8,128)} %bitcast.10, s32[2,32]{1,0:T(2,128)} %bitcast.12), custom_call_target="tpu_custom_call" | custom-call | flops 6442450944 | bytes 1048576 | tf_op jit(solution)/shard_map/sample/pallas_call | solution.py:430
  17.4 0.0 copy-done
  17.5 0.0 copy-done.1
  17.5 0.0 copy-start.2
  17.5 4.4 %join.1 = (f32[32,64,128]{2,1,0:T(8,128)S(1)}, f32[32,64,128]{2,1,0:T(8,128)}, f32[64,128]{1,0:T(8,128)S(1)}) custom-call(s32[32,2,128]{2,1,0:T(2,128)S(1)} %get-tuple-element.7.ids_ref, s32[1]{0:T(128)} %bitcast.5.side_ref, f32[32,6,128]{2,1,0:T(8,128)S(1)} %get-tuple-element.8.got_ref, f32[32,64,128]{2,1,0:T(8,128)S(1)} %copy-done, ...), custom_call_target="tpu_custom_call" | custom-call | tf_op jit(solution)/shard_map/join/pallas_call | solution.py:455
  21.9 0.0 copy-done.2
  21.9 16.7 %refine.1 = f32[32,64,128]{2,1,0:T(8,128)S(1)} custom-call(f32[32,64,128]{2,1,0:T(8,128)S(1)} %get-tuple-element.9.joined_ref, f32[64,128]{1,0:T(8,128)S(1)} %get-tuple-element.10.packed_ref, bf16[3,3,3,16,64]{4,3,2,1,0:T(8,128)(2,1)S(1)} %bitcast.8), custom_call_target="tpu_custom_call" | custom-call | tf_op jit(solution)/shard_map/refine/pallas_call | solution.py:465
  38.7 1.0 %copy.10 = f32[32,64,128]{2,1,0:T(8,128)} copy(f32[32,64,128]{2,1,0:T(8,128)S(1)} %refine.1) | data formatting | bytes 2097152
Async XLA Ops:
  0.6 16.8 %copy-start = (f32[32,64,128]{2,1,0:T(8,128)S(1)}, f32[32,64,128]{2,1,0:T(8,128)}, u32[]{:S(2)}) copy-start(f32[32,64,128]{2,1,0:T(8,128)} %prior_ref.1) | copy-start | bytes 3145732
  0.6 16.8 %copy-start.1 = (f32[32,64,128]{2,1,0:T(8,128)S(1)}, f32[32,64,128]{2,1,0:T(8,128)}, u32[]{:S(2)}) copy-start(f32[32,64,128]{2,1,0:T(8,128)} %weight_ref.1) | copy-start | bytes 3145732
  17.5 4.5 %copy-start.2 = (bf16[3,64,16,3,3]{1,2,4,3,0:T(8,128)(2,1)S(1)}, bf16[3,64,16,3,3]{1,2,4,3,0:T(8,128)(2,1)}, u32[]{:S(2)}) copy-start(bf16[3,64,16,3,3]{1,2,4,3,0:T(8,128)(2,1)} %param.13) | copy-start | bytes 165892

commit v3 on v2

--- a/solution.py
+++ b/solution.py
@@ -11,6 +11,7 @@
 TRUNC = 4
 LANES = 128
 VMEM = pltpu.VMEM
+CORNER = 16
 UNROLL_ROWS = 4
 
 
@@ -114,7 +115,8 @@
     ids_ref[...] = got_ref[:, 2 * cap : 3 * cap, :].astype(jnp.int32)
 
 
-def join_kernel(halo, ids_ref, side_ref, got_ref, prior_ref, weight_ref, joined_ref, total_ref, packed_ref):
+def join_kernel(halo, ids_ref, side_ref, got_ref, prior_ref, weight_ref, joined_ref, total_ref, packed_ref,
+                edge_ref, corner_ref):
     tiles, bins, cols = prior_ref.shape
     readers, rows, _ = got_ref.shape
     cap = rows // 3
@@ -164,11 +166,18 @@
         here = (place >= halo * t) & (place < halo * t + halo)
         return jnp.where(here, moved, packed)
 
-    packed_ref[...] = lax.fori_loop(0, tiles, finish, jnp.zeros((bins, cols), jnp.float32), unroll=4)
-
-
-def refine_kernel(layers, joined_ref, packed_ref, kernel_ref, out_ref,
-                  edge_rows, edge_cols, cur_ref, even_ref, odd_ref, weights_ref, side_weights_ref,
+    packed = lax.fori_loop(0, tiles, finish, jnp.zeros((bins, cols), jnp.float32), unroll=4)
+    packed_ref[...] = packed
+    for i in range(halo):
+        edge_ref[0, i] = joined_ref[i].astype(jnp.bfloat16)
+        edge_ref[1, i] = joined_ref[tiles - halo + i].astype(jnp.bfloat16)
+    turned = packed.T
+    corner_ref[0] = turned[0:CORNER].astype(jnp.bfloat16)
+    corner_ref[1] = turned[halo * tiles - CORNER : halo * tiles].astype(jnp.bfloat16)
+
+
+def refine_kernel(layers, joined_ref, packed_ref, edge_ref, corner_ref, kernel_ref, out_ref,
+                  edge_rows, edge_cols, corners, cur_ref, even_ref, odd_ref, weights_ref, side_weights_ref,
                   side_ref, gap_ref, send_sems, recv_sems):
     tiles, bins, cols = joined_ref.shape
     halo = layers
@@ -201,15 +210,11 @@
             src_ref=source, dst_ref=target, send_sem=send_sems.at[slot], recv_sem=recv_sems.at[slot],
             device_id=device, device_id_type=pl.DeviceIdType.MESH)
 
-    leading = joined_ref.at[0:halo]
-    trailing = joined_ref.at[tiles - halo : tiles]
-    to_side = copy(packed_ref, edge_cols.at[0], 2, (row, other))
-    to_down = [copy(packed_ref, edge_cols.at[1], 3, (row + 1, other)),
-               copy(packed_ref, edge_cols.at[3], 5, (row + 1, col)),
-               copy(trailing, edge_rows.at[0], 0, (row + 1, col))]
-    to_up = [copy(packed_ref, edge_cols.at[2], 4, (row - 1, other)),
-             copy(packed_ref, edge_cols.at[4], 6, (row - 1, col)),
-             copy(leading, edge_rows.at[1], 1, (row - 1, col))]
+    to_side = copy(packed_ref, edge_cols, 2, (row, other))
+    to_down = [copy(corner_ref.at[1], corners.at[0], 3, (row + 1, other)),
+               copy(edge_ref.at[1], edge_rows.at[0], 0, (row + 1, col))]
+    to_up = [copy(corner_ref.at[0], corners.at[1], 4, (row - 1, other)),
+             copy(edge_ref.at[0], edge_rows.at[1], 1, (row - 1, col))]
     to_side.start()
 
     @pl.when(has_up)
@@ -275,36 +280,41 @@
     side_col = jnp.where(first, 1 - halo, 0)
     shift_in = [one + jnp.where(m, mine_col, side_col) for one, m in zip(spot_in, mine)]
 
-    def collect(own, neighbour, h, offset, low, high):
-        source = (place[h] - offset) * halo + shift_in[h]
-        source = jnp.minimum(jnp.maximum(source, 0), cols - 1)
-        value = jnp.where(mine[h], jnp.take_along_axis(own, source, axis=1),
-                          jnp.take_along_axis(neighbour, source, axis=1))
-        return value, (place[h] >= low) & (place[h] < high)
+    def lanes_of(value, source):
+        return jnp.take_along_axis(value, jnp.minimum(jnp.maximum(source, 0), cols - 1), axis=1)
 
     to_side.wait_recv()
     for h in range(len(place)):
-        value, here = collect(packed_ref[...], edge_cols[0], h, halo, halo, halo + tiles)
+        source = (place[h] - halo) * halo + shift_in[h]
+        value = jnp.where(mine[h], lanes_of(packed_ref[...], source), lanes_of(edge_cols[...], source))
+        here = (place[h] >= halo) & (place[h] < halo + tiles)
         side_ref[:, h * cols : (h + 1) * cols] = jnp.where(here, value, 0.0)
     outer = jnp.zeros((bins, cols), jnp.bfloat16)
     odd_ref[0:bins, :] = outer
     odd_ref[(total - 1) * bins : total * bins, :] = outer
     nothing = jnp.zeros((bins, cols), jnp.float32)
 
-    def join_side(own, neighbour, offset, low, high):
+    own_col = jnp.where(first, cols - halo + 1, -halo)
+
+    def join_side(edge, corner, base, low):
+        turned = jnp.concatenate([corner.astype(jnp.float32), jnp.zeros((cols - CORNER, bins), jnp.float32)], axis=0).T
         for h in range(len(place)):
-            if low < (h + 1) * cols // span + 1 and high > h * cols // span:
-                value, here = collect(own, neighbour, h, offset, low, high)
+            if low <= ((h + 1) * cols - 1) // span and low + halo > h * cols // span:
                 part = side_ref[:, h * cols : (h + 1) * cols]
-                side_ref[:, h * cols : (h + 1) * cols] = jnp.where(here, value, part)
+                here = jnp.logical_not(mine[h]) & (place[h] >= low) & (place[h] < low + halo)
+                part = jnp.where(here, lanes_of(turned, (place[h] - low) * halo + base + shift_in[h]), part)
+                for i in range(halo):
+                    line = lanes_of(edge[i].astype(jnp.float32), spot_in[h] + own_col)
+                    part = jnp.where(mine[h] & (place[h] == low + i), line, part)
+                side_ref[:, h * cols : (h + 1) * cols] = part
 
     @pl.when(has_up)
     def _():
         for one in to_down:
             one.wait_recv()
-        join_side(edge_cols[3], edge_cols[1], halo - tiles, 0, halo)
+        join_side(edge_rows[0], corners[0], CORNER - halo * halo, 0)
         for i in range(halo):
-            put(i, edge_rows[0, i])
+            put(i, edge_rows[0, i].astype(jnp.float32))
 
     @pl.when(jnp.logical_not(has_up))
     def _():
@@ -315,9 +325,9 @@
     def _():
         for one in to_up:
             one.wait_recv()
-        join_side(edge_cols[4], edge_cols[2], halo + tiles, halo + tiles, total)
+        join_side(edge_rows[1], corners[1], 0, halo + tiles)
         for i in range(halo):
-            put(tiles + halo + i, edge_rows[1, i])
+            put(tiles + halo + i, edge_rows[1, i].astype(jnp.float32))
 
     @pl.when(jnp.logical_not(has_down))
     def _():
@@ -452,11 +462,14 @@
         pixel_index[0], depth_maps.reshape(-1, LANES), confidence.reshape(-1, LANES), frustum_tiles[0].T)))
     side = lax.axis_index("col").astype(jnp.int32).reshape(1)
     field = jax.ShapeDtypeStruct((tiles, bins, cols), f32)
-    joined, new_weight, packed = pl.pallas_call(
+    bf16 = jnp.bfloat16
+    joined, new_weight, packed, edge, corner = pl.pallas_call(
         functools.partial(join_kernel, layers),
-        out_shape=(field, field, jax.ShapeDtypeStruct((bins, cols), f32)),
+        out_shape=(field, field, jax.ShapeDtypeStruct((bins, cols), f32),
+                   jax.ShapeDtypeStruct((2, layers, bins, cols), bf16),
+                   jax.ShapeDtypeStruct((2, CORNER, bins), bf16)),
         in_specs=[pl.BlockSpec(memory_space=pltpu.SMEM)] * 2 + vmem_specs(3),
-        out_specs=tuple(vmem_specs(3)),
+        out_specs=tuple(vmem_specs(5)),
         compiler_params=pltpu.CompilerParams(vmem_limit_bytes=20 << 20),
         name="join",
     )(ids, side, got, tsdf_prior, prior_weight)
@@ -465,11 +478,12 @@
     refined = pl.pallas_call(
         functools.partial(refine_kernel, layers),
         out_shape=field,
-        in_specs=vmem_specs(3),
+        in_specs=vmem_specs(5),
         out_specs=pl.BlockSpec(memory_space=VMEM),
         scratch_shapes=[
-            VMEM((2, layers, bins, cols), f32),
-            VMEM((5, bins, cols), f32),
+            VMEM((2, layers, bins, cols), bf16),
+            VMEM((bins, cols), f32),
+            VMEM((2, CORNER, bins), bf16),
             VMEM((total_rows * bins, cols), f32),
             VMEM((total_rows * bins, cols), jnp.bfloat16),
             VMEM((total_rows * bins, cols), jnp.bfloat16),
@@ -477,12 +491,12 @@
             VMEM((layers, 2 * bins, 9 * bins), jnp.bfloat16),
             VMEM((bins, wide), f32),
             VMEM((layers, bins, cols), f32),
-            pltpu.SemaphoreType.DMA((7,)),
-            pltpu.SemaphoreType.DMA((7,)),
+            pltpu.SemaphoreType.DMA((5,)),
+            pltpu.SemaphoreType.DMA((5,)),
         ],
         compiler_params=pltpu.CompilerParams(collective_id=0, has_side_effects=True, vmem_limit_bytes=20 << 20),
         name="refine",
-    )(joined, packed, conv_weights.transpose(0, 3, 4, 2, 1))
+    )(joined, packed, edge, corner, conv_weights.transpose(0, 3, 4, 2, 1))
     return (refined, new_weight)
 
 

time: 39.8 us -> 35.5 us (0.89)
  Pallas kernels: 38 us -> 33.4 us
    pallas_call x1, Pallas kernels: 16.7 us -> 12.2 us  [on_device(): pl.pallas_call(functools.partial(refine_kernel, layers), out_shape=field,...]
where the time goes in v3:
time: 35.5 us; the launch traced here: 35.1 us
  Pallas kernels  33.4 us (94%)
  local copies, waits for them, and re-layouts  0.99 us (3%)
  between operations  0.69 us (2%)
    pallas_call x1, Pallas kernels, on_device(): pl.pallas_call(sample_kernel, out_shape=(jax.ShapeDtypeStruct((owners, 3...  16.8 us
    pallas_call x1, Pallas kernels, on_device(): pl.pallas_call(functools.partial(refine_kernel, layers), out_shape=field,...  12.2 us
    pallas_call x1, Pallas kernels, on_device(): pl.pallas_call(functools.partial(join_kernel, layers), out_shape=(field,...  4.42 us
    unnamed x7, local copies, waits for them, and re-layouts  0.99 us

profile of v3, /device:TPU:11, one launch (start us, length us, event | category | flops | bytes accessed | tf_op | source)
XLA Modules:
  0.0 35.1 jit_solution(13114031268936424510)
XLA Ops:
  0.6 0.0 copy-start
  0.6 0.0 copy-start.1
  0.7 16.8 %sample.1 = (f32[32,6,128]{2,1,0:T(8,128)S(1)}, s32[32,2,128]{2,1,0:T(2,128)S(1)}) custom-call(s32[32,2,128]{2,1,0:T(2,128)} %bitcast.11, f32[1024,128]{1,0:T(8,128)} %bitcast.9, f32[1024,128]{1,0:T(8,128)} %bitcast.10, s32[2,32]{1,0:T(2,128)} %bitcast.12), custom_call_target="tpu_custom_call" | custom-call | flops 6442450944 | bytes 1048576 | tf_op jit(solution)/shard_map/sample/pallas_call | solution.py:440
  17.4 0.0 copy-done
  17.5 0.0 copy-done.1
  17.5 0.0 copy-start.2
  17.5 4.4 %join.1 = (f32[32,64,128]{2,1,0:T(8,128)S(1)}, f32[32,64,128]{2,1,0:T(8,128)}, f32[64,128]{1,0:T(8,128)S(1)}, bf16[2,3,64,128]{3,2,1,0:T(8,128)(2,1)S(1)}, bf16[2,16,64]{2,1,0:T(8,128)(2,1)S(1)}) custom-call(s32[32,2,128]{2,1,0:T(2,128)S(1)} %get-tuple-element.9.ids_ref, s32[1]{0:T(128)} %bitcast.5.side_ref, f32[32,6,128]{2,1,0:T(8,128)S(1)} %get-tuple-element.10.got_ref, ...), custom_call_target="tpu_custom_call" | custom-call | tf_op jit(solution)/shard_map/join/pallas_call | solution.py:466
  21.9 0.0 copy-done.2
  21.9 12.2 %refine.1 = f32[32,64,128]{2,1,0:T(8,128)S(1)} custom-call(f32[32,64,128]{2,1,0:T(8,128)S(1)} %get-tuple-element.11.joined_ref, f32[64,128]{1,0:T(8,128)S(1)} %get-tuple-element.12.packed_ref, bf16[2,3,64,128]{3,2,1,0:T(8,128)(2,1)S(1)} %get-tuple-element.13.edge_ref, bf16[2,16,64]{2,1,0:T(8,128)(2,1)S(1)} %get-tuple-element.14.corner_ref, ...), custom_call_target="tpu_custom_call" | custom-call | tf_op jit(solution)/shard_map/refine/pallas_call | solution.py:478
  34.1 1.0 %copy.10 = f32[32,64,128]{2,1,0:T(8,128)} copy(f32[32,64,128]{2,1,0:T(8,128)S(1)} %refine.1) | data formatting | bytes 2097152
Async XLA Ops:
  0.6 16.8 %copy-start = (f32[32,64,128]{2,1,0:T(8,128)S(1)}, f32[32,64,128]{2,1,0:T(8,128)}, u32[]{:S(2)}) copy-start(f32[32,64,128]{2,1,0:T(8,128)} %prior_ref.1) | copy-start | bytes 3145732
  0.6 16.8 %copy-start.1 = (f32[32,64,128]{2,1,0:T(8,128)S(1)}, f32[32,64,128]{2,1,0:T(8,128)}, u32[]{:S(2)}) copy-start(f32[32,64,128]{2,1,0:T(8,128)} %weight_ref.1) | copy-start | bytes 3145732
  17.5 4.4 %copy-start.2 = (bf16[3,64,16,3,3]{1,2,4,3,0:T(8,128)(2,1)S(1)}, bf16[3,64,16,3,3]{1,2,4,3,0:T(8,128)(2,1)}, u32[]{:S(2)}) copy-start(bf16[3,64,16,3,3]{1,2,4,3,0:T(8,128)(2,1)} %param.13) | copy-start | bytes 165892
